TPU v7x, 768 devices: a whole 4x8x12 slice. The times are simulated.
768 devices in a mesh: row: 96 (over z, y_lo, core), col: 8 (over x, y_hi).
Axes of the slice: x: 4, y: 8 (y_hi: 2, y_lo: 4; y = y_hi * 4 + y_lo), z: 12, core: 2. Of those that a mesh axis runs over, the one named last changes fastest.
Arguments:
- specimen: float32 [2, 12288, 1024], P(None, 'row', 'col'), may hold values from -4 to 4
- probe_mode_stack: float32 [4, 2, 256, 256], replicated, may hold values from -4 to 4
- measured: float32 [96, 8, 1, 256, 256], P('row', 'col'), may hold values from 0.3 to 3
- centers: int32 [96, 8, 2, 2], P('row', 'col'), may hold values from 1 to 127
- frame_counts: int32 [96, 8], P('row', 'col'), may hold values from 0 to 2, as said below
- helper_cols: int32 [96, 8, 2], P('row', 'col'), may hold values from 0 to 7, as said below
Outputs:
- gradient: float32 [2, 12288, 1024], P(None, 'row', 'col')
Inputs may be any that keep to these rules, and one draw needn't show every extreme that they name: `frame_counts`: in every row of tiles the counts sum to 1 times the number of tiles in the row, and some tile of every row holds 2 frames. `helper_cols`: among a tile's live slots the helper columns are distinct; in every row of tiles each column is named by exactly one live slot; slots past a tile's count hold arbitrary columns.
All inputs are finite; a program needn't handle non-finite values.
Results may differ from a plain program's by a relative error of at most 0.007.
Values may be sent and summed in bfloat16 or wider, within the bound.
A program may use at most 32 MiB of HBM per device.

v0:
```python
import math

import jax
import jax.numpy as jnp
from jax import lax
from jax.sharding import PartitionSpec as P


def extended(block, sides, width):
    for axis, dim in sides:
        count = lax.axis_size(axis)
        forward = [(i, i + 1) for i in range(count - 1)]
        backward = [(target, source) for source, target in forward]
        low = lax.ppermute(
            lax.slice_in_dim(block, block.shape[dim] - width, None, axis=dim), axis, forward
        )
        high = lax.ppermute(lax.slice_in_dim(block, 0, width, axis=dim), axis, backward)
        block = jnp.concatenate([low, block, high], axis=dim)
    return block


def dft_tables(extent):
    steps_idx = jnp.arange(extent, dtype=jnp.int32)
    product = steps_idx[:, None] * steps_idx[None, :] % extent
    angles = product.astype(jnp.float32) * (2.0 * math.pi / extent)
    scaling = 1.0 / math.sqrt(extent)
    return (
        (jnp.cos(angles) * scaling).astype(jnp.bfloat16),
        (-jnp.sin(angles) * scaling).astype(jnp.bfloat16),
    )


def right_apply(operand, fourier_real_table, fourier_imaginary_table, conj_sign):
    extent = fourier_real_table.shape[0]
    joined = jnp.concatenate([fourier_real_table, fourier_imaginary_table], axis=1)
    products = jnp.einsum("bxy,yv->bxv", operand, joined, preferred_element_type=jnp.float32)
    real_part = products[:, :extent, :extent] - conj_sign * products[:, extent:, extent:]
    imag_part = products[:, extent:, :extent] + conj_sign * products[:, :extent, extent:]
    return jnp.concatenate([real_part, imag_part], axis=1)


def left_apply(operand, fourier_real_table, fourier_imaginary_table, conj_sign):
    upper_rows = jnp.concatenate([fourier_real_table, -conj_sign * fourier_imaginary_table], axis=1)
    lower_rows = jnp.concatenate([conj_sign * fourier_imaginary_table, fourier_real_table], axis=1)
    mixer_matrix = jnp.concatenate([upper_rows, lower_rows], axis=0)
    return jnp.einsum("uv,bvc->buc", mixer_matrix, operand, preferred_element_type=jnp.float32)


def per_frame_gradients(
    object_patches, probe_mode_stack, measured, fourier_real_table, fourier_imaginary_table
):
    helper_slot_count = object_patches.shape[0]
    extent = object_patches.shape[2]
    mode_count = probe_mode_stack.shape[0]
    patch_re = object_patches[:, None, :extent].astype(jnp.float32)
    patch_im = object_patches[:, None, extent:].astype(jnp.float32)
    probe_re = probe_mode_stack[None, :, 0]
    probe_im = probe_mode_stack[None, :, 1]
    exit_wave = jnp.concatenate(
        [probe_re * patch_re - probe_im * patch_im, probe_re * patch_im + probe_im * patch_re],
        axis=2,
    )
    exit_wave = exit_wave.astype(jnp.bfloat16).reshape(
        helper_slot_count * mode_count, 2 * extent, extent
    )
    half_wave = right_apply(exit_wave, fourier_real_table, fourier_imaginary_table, 1.0).astype(
        jnp.bfloat16
    )
    far_field = left_apply(half_wave, fourier_real_table, fourier_imaginary_table, 1.0).reshape(
        helper_slot_count, mode_count, 2 * extent, extent
    )
    far_re = far_field[:, :, :extent]
    far_im = far_field[:, :, extent:]
    intensity = jnp.sum(far_re * far_re + far_im * far_im, axis=1)
    factor = 1.0 - measured / jnp.sqrt(jnp.maximum(intensity, 0.25))
    doubled = jnp.concatenate([factor, factor], axis=1)[:, None]
    corrected = (
        (far_field * doubled)
        .astype(jnp.bfloat16)
        .reshape(helper_slot_count * mode_count, 2 * extent, extent)
    )
    back_half = right_apply(corrected, fourier_real_table, fourier_imaginary_table, -1.0).astype(
        jnp.bfloat16
    )
    inverse = left_apply(back_half, fourier_real_table, fourier_imaginary_table, -1.0).reshape(
        helper_slot_count, mode_count, 2 * extent, extent
    )
    chi_re = inverse[:, :, :extent]
    chi_im = inverse[:, :, extent:]
    grad_re = jnp.sum(probe_re * chi_re + probe_im * chi_im, axis=1)
    grad_im = jnp.sum(probe_re * chi_im - probe_im * chi_re, axis=1)
    return jnp.concatenate([grad_re, grad_im], axis=1).astype(jnp.bfloat16)


def fold_axis(spread, axis_dim, windows):
    result = None
    for window in windows:
        portion = lax.slice_in_dim(spread, window[0], window[0] + window[2], axis=axis_dim)
        result = portion if result is None else result + portion
    return result


def slot_picker(present, helper_slot_count):
    ranking = jnp.cumsum(present) - present
    return present[:, None] * (
        ranking[:, None] == jnp.arange(helper_slot_count, dtype=jnp.int32)[None, :]
    ).astype(jnp.int32)


def per_device(specimen, probe_mode_stack, measured, centers, frame_counts, helper_cols):
    frame_side_length = probe_mode_stack.shape[-1]
    half_size = frame_side_length // 2
    tile_size = specimen.shape[1]
    capacity = centers.shape[2]
    helper_slot_count = measured.shape[2]
    helper_count = lax.axis_size("col")
    fourier_real_table, fourier_imaginary_table = dft_tables(frame_side_length)
    padded = extended(specimen.astype(jnp.bfloat16), (("row", 1), ("col", 2)), half_size).astype(
        specimen.dtype
    )
    local_centers = centers.reshape(capacity, 2)
    local_targets = helper_cols.reshape(capacity)
    local_count = frame_counts.reshape(())
    pieces = []
    for slot_idx in range(capacity):
        corner = (jnp.int32(0), local_centers[slot_idx, 0], local_centers[slot_idx, 1])
        pieces.append(
            lax.dynamic_slice(padded, corner, (2, frame_side_length, frame_side_length)).reshape(
                2 * frame_side_length, frame_side_length
            )
        )
    object_patches = jnp.stack(pieces).astype(jnp.bfloat16)
    is_live = jnp.arange(capacity, dtype=jnp.int32) < local_count
    helper_range = jnp.arange(helper_count, dtype=jnp.int32)
    routing = (local_targets[None, :] == helper_range[:, None]) & is_live[None, :]
    local_measurements = measured.reshape(helper_slot_count, frame_side_length, frame_side_length)
    route_mix = routing.astype(jnp.bfloat16)
    outgoing = jnp.einsum(
        "hj,jxy->hxy", route_mix, object_patches, preferred_element_type=jnp.float32
    ).astype(jnp.bfloat16)
    live_flags = jnp.sum(routing.astype(jnp.float32), axis=1, keepdims=True).astype(jnp.bfloat16)
    incoming, in_flags = (
        lax.all_to_all(outgoing, "col", split_axis=0, concat_axis=0, tiled=True),
        lax.all_to_all(live_flags, "col", split_axis=0, concat_axis=0, tiled=True),
    )
    present = (in_flags[:, 0] > 0.5).astype(jnp.int32)
    picker = slot_picker(present, helper_slot_count)
    sources = jnp.sum(picker * helper_range[:, None], axis=0)
    selected_frames = jnp.take(incoming, sources, axis=0)
    patch_gradients = per_frame_gradients(
        selected_frames,
        probe_mode_stack,
        local_measurements,
        fourier_real_table,
        fourier_imaginary_table,
    )
    returned = jnp.einsum(
        "hs,sxy->hxy",
        picker.astype(jnp.bfloat16),
        patch_gradients,
        preferred_element_type=jnp.float32,
    ).astype(jnp.bfloat16)
    answers = lax.all_to_all(returned, "col", split_axis=0, concat_axis=0, tiled=True)
    per_frame = jnp.einsum("hj,hxy->jxy", route_mix, answers, preferred_element_type=jnp.float32)
    padded_size = tile_size + 2 * half_size
    grad_pad = jnp.zeros((2, padded_size, padded_size), jnp.float32)
    for slot_idx in range(capacity):
        corner = (jnp.int32(0), local_centers[slot_idx, 0], local_centers[slot_idx, 1])
        current = lax.dynamic_slice(grad_pad, corner, (2, frame_side_length, frame_side_length))
        added = current + per_frame[slot_idx].reshape(2, frame_side_length, frame_side_length)
        grad_pad = lax.dynamic_update_slice(grad_pad, added, corner)
    windows = (
        (0, 0, half_size),
        (2 * half_size, 0, tile_size),
        (padded_size + half_size, tile_size - half_size, half_size),
    )
    spread = extended(grad_pad, (("row", 1), ("col", 2)), half_size)
    return fold_axis(fold_axis(spread, 1, windows), 2, windows)


def solution(mesh):
    return jax.shard_map(
        per_device,
        mesh=mesh,
        in_specs=(
            P(None, "row", "col"),
            P(),
            P("row", "col", None, None, None),
            P("row", "col", None, None),
            P("row", "col"),
            P("row", "col", None),
        ),
        out_specs=P(None, "row", "col"),
        check_vma=False,
    )
```

profile of v0, /device:TPU:80, one launch (start us, length us, event | category | flops | bytes accessed | tf_op | source)
XLA Modules:
  0.0 260.5 jit_solution(12044013356369178208)
XLA Ops:
  0.0 0.9 convert_element_type.142
  0.9 1.9 collective-permute-start
  2.8 3.6 %collective-permute-start.1 = (bf16[2,128,128]{2,1,0:T(8,128)(2,1)S(1)}, bf16[2,128,128]{2,1,0:T(8,128)(2,1)S(1)}, u32[]{:S(2)}, u32[]{:S(2)}) collective-permute-start(bf16[2,128,128]{2,1,0:T(8,128)(2,1)S(1)} %convert_element_type.142), channel_id=1, source_target_pairs={{8,0},{16,8},{24,16},{32,24},{40,32},{48,40},{56,48},{64,56},{72,6... | collective-permute-start | bytes 196616 | tf_op jit(solution)/shard_map/ppermute | solution.py:17
  7.2 0.0 copy-start.2
  7.2 0.0 collective-permute-done
  7.2 1.2 collective-permute-done.1
  8.4 6.2 %collective-permute-start.2 = (bf16[2,384,128]{2,1,0:T(8,128)(2,1)S(1)}, bf16[2,384,128]{2,1,0:T(8,128)(2,1)S(1)}, u32[]{:S(2)}, u32[]{:S(2)}) collective-permute-start(bf16[2,384,128]{2,1,0:T(8,128)(2,1)S(1)} %pad_maximum_fusion.9), channel_id=1, source_target_pairs={{0,1},{1,2},{2,3},{3,4},{4,5},{5,6},{6,7},{8,9},{9,10},{10,11},{11... | collective-permute-start | bytes 589832 | tf_op jit(solution)/shard_map/ppermute | solution.py:14
  14.6 1.3 collective-permute-start.3
  15.9 0.7 convert_reduce_fusion
  16.7 0.7 copy.35
  17.4 10.3 %all-to-all-start = ((bf16[8,1,1]{2,1,0:T(2,128)(2,1)}), bf16[8,1,1]{2,1,0:T(2,128)(2,1)S(1)}, u32[]{:S(2)}, u32[]{:S(2)}) async-start(bf16[8,1,1]{2,1,0:T(2,128)(2,1)} %copy.35), calls=%async_computation | async-start | bytes 8192 | tf_op jit(solution)/shard_map/all_to_all | solution.py:144
  27.6 1.5 fusion.72
  36.6 0.0 collective-permute-done.2
  36.6 0.0 collective-permute-done.3
  36.6 0.1 maximum_convert_fusion
  36.7 0.3 dynamic-slice_convert_fusion.1
  37.0 0.4 copy.37
  37.5 0.4 copy.38
  37.9 0.0 copy-done.2
  37.9 1.8 convolution_convert_fusion
  39.7 1.7 copy.39
  41.4 0.0 copy-start.1
  41.4 0.0 all-to-all-done
  41.4 9.7 %all-to-all-start.1 = ((bf16[8,512,256]{2,1,0:T(8,128)(2,1)}), bf16[8,512,256]{2,1,0:T(8,128)(2,1)}, u32[]{:S(2)}, u32[]{:S(2)}) async-start(bf16[8,512,256]{2,1,0:T(8,128)(2,1)} %copy.39), calls=%async_computation.1 | async-start | bytes 4194304 | tf_op jit(solution)/shard_map/all_to_all | solution.py:143
  51.2 0.0 copy-done.1
  51.2 0.0 copy-start
  51.2 0.1 copy.42
  51.3 1.0 broadcast_multiply_fusion
  52.3 1.1 multiply_convert_fusion.1
  53.4 0.2 fusion.58
  53.7 0.2 reduce-window.4
  53.9 0.6 fusion.64
  56.5 48.2 %all-to-all-done.1 = bf16[8,512,256]{2,1,0:T(8,128)(2,1)} async-done(((bf16[8,512,256]{2,1,0:T(8,128)(2,1)}), bf16[8,512,256]{2,1,0:T(8,128)(2,1)}, u32[]{:S(2)}, u32[]{:S(2)}) %all-to-all-start.1) | async-done | bytes 2097184 | tf_op jit(solution)/shard_map/all_to_all | solution.py:143
  104.6 1.0 dynamic-slice_select_fusion
  105.6 0.0 copy-done
  105.7 0.3 fusion.29
  106.0 0.7 fusion.13
  106.7 0.3 fusion.12
  106.9 0.8 fusion.17
  107.7 0.1 fusion.10
  108.0 0.8 fusion.3
  108.7 0.4 fusion.8
  109.1 0.7 convolution_bitcast_fusion
  109.8 0.4 fusion.25
  110.3 0.7 multiply_convert_fusion
  111.0 46.2 %all_to_all.16 = bf16[8,512,256]{2,1,0:T(8,128)(2,1)S(1)} all-to-all(bf16[8,512,256]{2,1,0:T(8,128)(2,1)S(1)} %multiply_convert_fusion), channel_id=1, replica_groups=mesh['row'=96,'col'=8] {'col'}, dimensions={0} | all-to-all | bytes 4194304 | tf_op jit(solution)/shard_map/all_to_all | solution.py:163
  157.2 1.5 fusion.1
  158.7 0.8 fusion.71
  159.6 0.1 broadcast_in_dim.11
  159.7 7.6 %dynamic_update_slice.6 = f32[2,384,384]{2,1,0:T(8,128)S(1)} dynamic-update-slice(f32[2,384,384]{2,1,0:T(8,128)S(1)} %broadcast_in_dim.11, f32[2,256,256]{2,1,0:T(8,128)S(1)} %bitcast.111, s32[]{:T(128)} %constant.23.clone.1, s32[]{:T(128)S(6)} %select_n.57, s32[]{:T(128)S(6)} %select_n.58) | dynamic-update-slice | bytes 1048580 | tf_op jit(solution)/shard_map/dynamic_update_slice | solution.py:171
  167.2 0.2 dynamic-slice_add_fusion
  167.5 7.9 %dynamic_update_slice.7 = f32[2,384,384]{2,1,0:T(8,128)S(1)} dynamic-update-slice(f32[2,384,384]{2,1,0:T(8,128)S(1)} %dynamic_update_slice.6, f32[2,256,256]{2,1,0:T(8,128)S(1)} %dynamic-slice_add_fusion, s32[]{:T(128)} %constant.23.clone.1, s32[]{:T(128)S(6)} %select_n.59, s32[]{:T(128)S(6)} %select_n.60) | dynamic-update-slice | bytes 1048580 | tf_op jit(solution)/shard_map/dynamic_update_slice | solution.py:171
  175.4 0.1 fusion.70
  175.4 1.9 collective-permute-start.4
  177.3 3.6 %collective-permute-start.5 = (f32[2,128,384]{2,1,0:T(8,128)S(1)}, f32[2,128,384]{2,1,0:T(8,128)S(1)}, u32[]{:S(2)}, u32[]{:S(2)}) collective-permute-start(f32[2,128,384]{2,1,0:T(8,128)S(1)} %get-tuple-element.27), channel_id=1, source_target_pairs={{8,0},{16,8},{24,16},{32,24},{40,32},{48,40},{56,48},{64,56},{72,6... | collective-permute-start | bytes 1179656 | tf_op jit(solution)/shard_map/ppermute | solution.py:17
  181.0 14.0 %collective-permute-done.4 = f32[2,128,384]{2,1,0:T(8,128)S(1)} collective-permute-done((f32[2,128,384]{2,1,0:T(8,128)S(1)}, f32[2,128,384]{2,1,0:T(8,128)S(1)}, u32[]{:S(2)}, u32[]{:S(2)}) %collective-permute-start.4) | collective-permute-done | bytes 393248 | tf_op jit(solution)/shard_map/ppermute | solution.py:14
  195.0 0.0 collective-permute-done.5
  195.0 0.1 pad_maximum_fusion.6
  195.1 1.3 collective-permute-start.6
  196.5 1.3 collective-permute-start.7
  197.8 10.1 %collective-permute-done.6 = f32[2,640,128]{2,1,0:T(8,128)S(1)} collective-permute-done((f32[2,640,128]{2,1,0:T(8,128)S(1)}, f32[2,640,128]{2,1,0:T(8,128)S(1)}, u32[]{:S(2)}, u32[]{:S(2)}) %collective-permute-start.6) | collective-permute-done | bytes 655392 | tf_op jit(solution)/shard_map/ppermute | solution.py:14
  207.9 51.9 %collective-permute-done.7 = f32[2,640,128]{2,1,0:T(8,128)S(1)} collective-permute-done((f32[2,640,128]{2,1,0:T(8,128)S(1)}, f32[2,640,128]{2,1,0:T(8,128)S(1)}, u32[]{:S(2)}, u32[]{:S(2)}) %collective-permute-start.7) | collective-permute-done | bytes 655392 | tf_op jit(solution)/shard_map/ppermute | solution.py:17
  259.7 0.7 fusion.54
  (9 shorter events, 0.3 us)
Async XLA Ops:
  0.9 6.3 %collective-permute-start = (bf16[2,128,128]{2,1,0:T(8,128)(2,1)S(1)}, bf16[2,128,128]{2,1,0:T(8,128)(2,1)S(1)}, u32[]{:S(2)}, u32[]{:S(2)}) collective-permute-start(bf16[2,128,128]{2,1,0:T(8,128)(2,1)S(1)} %convert_element_type.142), channel_id=1, source_target_pairs={{0,8},{8,16},{16,24},{24,32},{32,40},{40,48},{48,56},{56,64},{64,7... | collective-permute-start | bytes 196616 | tf_op jit(solution)/shard_map/ppermute | solution.py:14
  2.8 5.5 %collective-permute-start.1 = (bf16[2,128,128]{2,1,0:T(8,128)(2,1)S(1)}, bf16[2,128,128]{2,1,0:T(8,128)(2,1)S(1)}, u32[]{:S(2)}, u32[]{:S(2)}) collective-permute-start(bf16[2,128,128]{2,1,0:T(8,128)(2,1)S(1)} %convert_element_type.142), channel_id=1, source_target_pairs={{8,0},{16,8},{24,16},{32,24},{40,32},{48,40},{56,48},{64,56},{72,6... | collective-permute-start | bytes 196616 | tf_op jit(solution)/shard_map/ppermute | solution.py:17
  7.2 30.7 %copy-start.2 = (s32[1,1,2]{2,1,0:T(1,128)S(1)}, s32[1,1,2]{2,1,0:T(1,128)}, u32[]{:S(2)}) copy-start(s32[1,1,2]{2,1,0:T(1,128)} %param.11) | copy-start | bytes 28
  8.4 28.2 %collective-permute-start.2 = (bf16[2,384,128]{2,1,0:T(8,128)(2,1)S(1)}, bf16[2,384,128]{2,1,0:T(8,128)(2,1)S(1)}, u32[]{:S(2)}, u32[]{:S(2)}) collective-permute-start(bf16[2,384,128]{2,1,0:T(8,128)(2,1)S(1)} %pad_maximum_fusion.9), channel_id=1, source_target_pairs={{0,1},{1,2},{2,3},{3,4},{4,5},{5,6},{6,7},{8,9},{9,10},{10,11},{11... | collective-permute-start | bytes 589832 | tf_op jit(solution)/shard_map/ppermute | solution.py:14
  14.6 22.0 %collective-permute-start.3 = (bf16[2,384,128]{2,1,0:T(8,128)(2,1)S(1)}, bf16[2,384,128]{2,1,0:T(8,128)(2,1)S(1)}, u32[]{:S(2)}, u32[]{:S(2)}) collective-permute-start(bf16[2,384,128]{2,1,0:T(8,128)(2,1)S(1)} %pad_maximum_fusion.9), channel_id=1, source_target_pairs={{1,0},{2,1},{3,2},{4,3},{5,4},{6,5},{7,6},{9,8},{10,9},{11,10},{12... | collective-permute-start | bytes 589832 | tf_op jit(solution)/shard_map/ppermute | solution.py:17
  17.4 24.1 %all-to-all-start = ((bf16[8,1,1]{2,1,0:T(2,128)(2,1)}), bf16[8,1,1]{2,1,0:T(2,128)(2,1)S(1)}, u32[]{:S(2)}, u32[]{:S(2)}) async-start(bf16[8,1,1]{2,1,0:T(2,128)(2,1)} %copy.35), calls=%async_computation | async-start | bytes 8192 | tf_op jit(solution)/shard_map/all_to_all | solution.py:144
  41.4 9.8 %copy-start.1 = (f32[1,1,1,256,256]{4,3,2,1,0:T(8,128)S(1)}, f32[1,1,1,256,256]{4,3,2,1,0:T(8,128)}, u32[]{:S(2)}) copy-start(f32[1,1,1,256,256]{4,3,2,1,0:T(8,128)} %param.8) | copy-start | bytes 786436
  41.4 63.2 %all-to-all-start.1 = ((bf16[8,512,256]{2,1,0:T(8,128)(2,1)}), bf16[8,512,256]{2,1,0:T(8,128)(2,1)}, u32[]{:S(2)}, u32[]{:S(2)}) async-start(bf16[8,512,256]{2,1,0:T(8,128)(2,1)} %copy.39), calls=%async_computation.1 | async-start | bytes 4194304 | tf_op jit(solution)/shard_map/all_to_all | solution.py:143
  51.2 54.5 %copy-start = (f32[4,2,256,256]{3,2,1,0:T(8,128)S(1)}, f32[4,2,256,256]{3,2,1,0:T(8,128)}, u32[]{:S(2)}) copy-start(f32[4,2,256,256]{3,2,1,0:T(8,128)} %param.7) | copy-start | bytes 6291460
  175.4 19.6 %collective-permute-start.4 = (f32[2,128,384]{2,1,0:T(8,128)S(1)}, f32[2,128,384]{2,1,0:T(8,128)S(1)}, u32[]{:S(2)}, u32[]{:S(2)}) collective-permute-start(f32[2,128,384]{2,1,0:T(8,128)S(1)} %get-tuple-element.26), channel_id=1, source_target_pairs={{0,8},{8,16},{16,24},{24,32},{32,40},{40,48},{48,56},{56,64},{64,7... | collective-permute-start | bytes 1179656 | tf_op jit(solution)/shard_map/ppermute | solution.py:14
  177.3 17.7 %collective-permute-start.5 = (f32[2,128,384]{2,1,0:T(8,128)S(1)}, f32[2,128,384]{2,1,0:T(8,128)S(1)}, u32[]{:S(2)}, u32[]{:S(2)}) collective-permute-start(f32[2,128,384]{2,1,0:T(8,128)S(1)} %get-tuple-element.27), channel_id=1, source_target_pairs={{8,0},{16,8},{24,16},{32,24},{40,32},{48,40},{56,48},{64,56},{72,6... | collective-permute-start | bytes 1179656 | tf_op jit(solution)/shard_map/ppermute | solution.py:17
  195.1 12.7 %collective-permute-start.6 = (f32[2,640,128]{2,1,0:T(8,128)S(1)}, f32[2,640,128]{2,1,0:T(8,128)S(1)}, u32[]{:S(2)}, u32[]{:S(2)}) collective-permute-start(f32[2,640,128]{2,1,0:T(8,128)S(1)} %get-tuple-element.24), channel_id=1, source_target_pairs={{0,1},{1,2},{2,3},{3,4},{4,5},{5,6},{6,7},{8,9},{9,10},{10,11},{11... | collective-permute-start | bytes 1966088 | tf_op jit(solution)/shard_map/ppermute | solution.py:14
  196.5 63.3 %collective-permute-start.7 = (f32[2,640,128]{2,1,0:T(8,128)S(1)}, f32[2,640,128]{2,1,0:T(8,128)S(1)}, u32[]{:S(2)}, u32[]{:S(2)}) collective-permute-start(f32[2,640,128]{2,1,0:T(8,128)S(1)} %get-tuple-element.25), channel_id=1, source_target_pairs={{1,0},{2,1},{3,2},{4,3},{5,4},{6,5},{7,6},{9,8},{10,9},{11,10},{12... | collective-permute-start | bytes 1966088 | tf_op jit(solution)/shard_map/ppermute | solution.py:17
where the time goes:
time: 261 us; the launch traced here: 260 us
  waiting for transfers between devices  125 us (48%)
  blocking collectives  46.2 us (18%)
  starting transfers between devices  41.3 us (16%)
  local copies, waits for them, and re-layouts  21.7 us (8%)
  between operations  10.4 us (4%)
  other arithmetic  9.27 us (4%)
  matrix products  6.23 us (2%)
    ppermute x4, waiting for transfers between devices, extended(): lax.ppermute(lax.slice_in_dim(block, 0, width, axis=dim), axis, backward)  53.1 us
    all_to_all x1, waiting for transfers between devices, per_device(): lax.all_to_all(outgoing, 'col', split_axis=0, concat_axis=0, tiled=True)  48.2 us
    all_to_all x1, blocking collectives, per_device(): lax.all_to_all(returned, 'col', split_axis=0, concat_axis=0, tiled=True)  46.2 us
    ppermute x4, waiting for transfers between devices, extended(): lax.ppermute(lax.slice_in_dim(block, block.shape[dim] - width, None, axis...  24.1 us
    dynamic_update_slice x2, local copies, waits for them, and re-layouts, per_device(): grad_pad = lax.dynamic_update_slice(grad_pad, added, corner)  15.5 us
    ppermute x4, starting transfers between devices, extended(): lax.ppermute(lax.slice_in_dim(block, block.shape[dim] - width, None, axis...  11.4 us
    all_to_all x1, starting transfers between devices, per_device(): lax.all_to_all(live_flags, 'col', split_axis=0, concat_axis=0, tiled=True)  10.3 us
    ppermute x4, starting transfers between devices, extended(): lax.ppermute(lax.slice_in_dim(block, 0, width, axis=dim), axis, backward)  9.87 us
  transfers between devices with their start and end apart: 10, of which 5 were waited for; matrix products, arithmetic and copies ran while one was open for 4% of the time, Pallas kernels for 0%

commit v1 on v0

v1 whole, which is shorter than its diff:
```python
import functools
import math

import jax
import jax.numpy as jnp
import numpy as np
from jax import lax
from jax.experimental import pallas as pl
from jax.experimental.pallas import tpu as pltpu
from jax.sharding import PartitionSpec as P

MESH = pl.DeviceIdType.MESH
F32 = jnp.float32
BF16 = jnp.bfloat16


def dft_blocks(extent):
    idx = np.arange(extent)
    angles = (idx[:, None] * idx[None, :] % extent) * (2.0 * math.pi / extent)
    scale = 1.0 / math.sqrt(extent)
    re, im = np.cos(angles) * scale, -np.sin(angles) * scale
    return np.block([[re, im], [-im, re]])


def dot(a, b):
    return jnp.dot(a, b, preferred_element_type=F32)


def kernel(
    n_r,
    n_c,
    centers,
    counts,
    helpers,
    spec,
    measured,
    probe_hbm,
    fwd_hbm,
    bwd_hbm,
    out,
    probe,
    fwd,
    bwd,
    meta,
    nb,
    meas,
    rows_buf,
    cols_buf,
    far,
    zbuf,
    g_own,
    g_on,
    g_off,
    g_sum,
    r_on_buf,
    r_buf,
    local_sem,
    meta_sem,
    halo_send,
    halo_recv,
    meas_send,
    meas_recv,
    grad_send,
    grad_recv,
):
    t = spec.shape[1]
    n = probe.shape[-1]
    modes = probe.shape[0]
    r, c = lax.axis_index("row"), lax.axis_index("col")
    odd_r, odd_c = lax.rem(r, 2), lax.rem(c, 2)
    r_on = r + 1 - 2 * odd_r
    r_off = lax.rem(r - 1 + 2 * odd_r + n_r, n_r)
    c_x = c + 1 - 2 * odd_c
    c_give = lax.rem(c - 2 + 4 * odd_c + n_c, n_c)
    c_take = lax.rem(c + 2 - 4 * odd_c + n_c, n_c)
    peers = [lax.rem(c + 2 * k, n_c) for k in range(1, n_c // 2)]

    barrier = pltpu.get_barrier_semaphore()
    partners = [(r_on, c), (r_off, c), (r, c_x), (r_off, c_x), (r_off, c_give), (r_off, c_take)]
    partners += [(r, p) for p in peers]
    for partner in partners:
        pl.semaphore_signal(barrier, inc=1, device_id=partner, device_id_type=MESH)

    loads = [
        pltpu.make_async_copy(src, dst, local_sem.at[i])
        for i, (src, dst) in enumerate([(probe_hbm, probe), (fwd_hbm, fwd), (bwd_hbm, bwd)])
    ]
    for load in loads:
        load.start()

    nb[0] = jnp.concatenate([spec[0], spec[1]], axis=1).astype(BF16)
    values = [centers[0], centers[1], centers[2], centers[3], helpers[0], helpers[1], counts[0]]
    which = lax.broadcasted_iota(jnp.int32, (8, 128), 0)
    block = jnp.zeros((8, 128), jnp.int32)
    for i, value in enumerate(values):
        block = jnp.where(which == i, value, block)
    meta[0] = block
    meas[c] = measured[...].astype(BF16)

    pl.semaphore_wait(barrier, len(partners))

    def remote(src, dst, send, recv, device):
        return pltpu.make_async_remote_copy(
            src_ref=src,
            dst_ref=dst,
            send_sem=send,
            recv_sem=recv,
            device_id=device,
            device_id_type=MESH,
        )

    def halo(src, dst, device):
        return remote(nb.at[src], nb.at[dst], halo_send.at[dst], halo_recv.at[dst], device)

    to_x = halo(0, 1, (r, c_x))
    to_off_x = halo(0, 7, (r_off, c_x))
    to_far = halo(0, 2, (r, c_give))
    to_off_far = halo(0, 8, (r_off, c_give))
    to_off = halo(0, 6, (r_off, c))
    to_on = halo(0, 3, (r_on, c))
    meta_copy = remote(meta.at[0], meta.at[1], meta_sem.at[0], meta_sem.at[1], (r, c_x))
    first = [meta_copy, to_x, to_off_x, to_off_far, to_far, to_off, to_on]
    for copy in first:
        copy.start()
    meas_x = remote(meas.at[c], meas.at[c], meas_send.at[0], meas_recv.at[0], (r, c_x))
    meas_x.start()
    meas_own = [
        remote(meas.at[c], meas.at[c], meas_send.at[k + 1], meas_recv.at[k + 1], (r, p))
        for k, p in enumerate(peers)
    ]
    for copy in meas_own:
        copy.start()

    to_x.wait_recv()
    fwd_x = halo(1, 4, (r_on, c))
    fwd_x.start()
    to_far.wait_recv()
    fwd_far = halo(2, 5, (r_on, c))
    fwd_far.start()

    meta_copy.wait_recv()
    info = meta[1]
    cr = [info[0:1, 0:1], info[2:3, 0:1]]
    cc = [info[1:2, 0:1], info[3:4, 0:1]]
    hc = [info[4:5, 0:1], info[5:6, 0:1]]
    live = [info[6:7, 0:1] > s for s in range(2)]

    nowhere = -4 * n
    row_on, row_off = 2 * t * (1 - odd_r), 2 * t * odd_r
    row_off = jnp.where((r == 0) | (r == n_r - 1), nowhere, row_off)
    col_own, col_far = 2 * t * odd_c, 2 * t * (1 - odd_c)
    col_far = jnp.where((c == 1) | (c == n_c - 2), nowhere, col_far)

    def place(idx, first_, second, third):
        role = idx // t
        base = jnp.where(role == 0, first_, jnp.where(role == 1, second, third))
        return base + idx - role * t

    def one_hot(shape, axis, roles, start):
        role_idx = lax.broadcasted_iota(jnp.int32, shape, axis)
        pix = lax.broadcasted_iota(jnp.int32, shape, 1 - axis)
        return jnp.where(place(role_idx, *roles) == pix + start, 1.0, 0.0).astype(BF16)

    row_roles = (t, row_on, row_off)
    col_roles = (col_own, t, col_far)
    row_at = [jnp.where(live[s], cr[s], 8 * n) for s in range(2)]

    for copy in (to_off, to_off_x, to_off_far, to_on, fwd_x, fwd_far):
        copy.wait_recv()
    for load in loads:
        load.wait()

    tiles = [jnp.concatenate([nb[j], nb[3 + j], nb[6 + j]], axis=0) for j in range(3)]

    for s in range(2):
        pick = one_hot((n, 3 * t), 1, row_roles, row_at[s])
        cut = [dot(pick, tiles[j]).astype(BF16) for j in range(3)]
        strip = jnp.concatenate(
            [
                jnp.concatenate([x[:, :t] for x in cut], axis=1),
                jnp.concatenate([x[:, t:] for x in cut], axis=1),
            ],
            axis=0,
        )
        patch = dot(strip, one_hot((3 * t, n), 0, col_roles, cc[s]))
        re, im = patch[:n], patch[n:]
        for k in range(modes):
            p_re, p_im = probe[k, 0], probe[k, 1]
            rows_buf[k * n : (k + 1) * n, :n] = (p_re * re - p_im * im).astype(BF16)
            rows_buf[k * n : (k + 1) * n, n:] = (p_re * im + p_im * re).astype(BF16)
        for k in range(modes):
            half = dot(rows_buf[k * n : (k + 1) * n], fwd[...]).astype(BF16)
            cols_buf[:n, k * n : (k + 1) * n] = half[:, :n]
            cols_buf[n:, k * n : (k + 1) * n] = half[:, n:]
        far[s] = dot(bwd[...], cols_buf[...])

    meas_x.wait_recv()
    meas_fwd = [
        remote(
            meas.at[c_x],
            meas.at[c_x],
            meas_send.at[n_c // 2 + k],
            meas_recv.at[n_c // 2 + k],
            (r, p),
        )
        for k, p in enumerate(peers)
    ]
    for copy in meas_fwd:
        copy.start()
    for copy in meas_own + meas_fwd:
        copy.wait_recv()

    for s in range(2):
        intensity = jnp.zeros((n, n), F32)
        for k in range(modes):
            f_re = far[s, :n, k * n : (k + 1) * n]
            f_im = far[s, n:, k * n : (k + 1) * n]
            intensity = intensity + (f_re * f_re + f_im * f_im)
        amp = jnp.zeros((n, n), F32)
        for h in range(n_c):
            amp = amp + jnp.where(hc[s] == h, meas[h].astype(F32), 0.0)
        factor = 1.0 - amp * lax.rsqrt(jnp.maximum(intensity, 0.25))
        for k in range(modes):
            for part in range(2):
                f = far[s, part * n : (part + 1) * n, k * n : (k + 1) * n]
                rows_buf[k * n : (k + 1) * n, part * n : (part + 1) * n] = (f * factor).astype(BF16)
        for k in range(modes):
            back = dot(rows_buf[k * n : (k + 1) * n], bwd[...]).astype(BF16)
            cols_buf[:n, k * n : (k + 1) * n] = back[:, :n]
            cols_buf[n:, k * n : (k + 1) * n] = back[:, n:]
        far[s] = dot(fwd[...], cols_buf[...])
        g_re = jnp.zeros((n, n), F32)
        g_im = jnp.zeros((n, n), F32)
        for k in range(modes):
            p_re, p_im = probe[k, 0], probe[k, 1]
            x_re = far[s, :n, k * n : (k + 1) * n]
            x_im = far[s, n:, k * n : (k + 1) * n]
            g_re = g_re + (p_re * x_re + p_im * x_im)
            g_im = g_im + (p_re * x_im - p_im * x_re)
        grad = jnp.concatenate([g_re, g_im], axis=0).astype(BF16)
        wide = dot(grad, one_hot((n, 3 * t), 1, col_roles, cc[s])).astype(BF16)
        for j in range(3):
            zbuf[j, s * n : (s + 1) * n, :t] = wide[:n, j * t : (j + 1) * t]
            zbuf[j, s * n : (s + 1) * n, t:] = wide[n:, j * t : (j + 1) * t]

    spread = jnp.concatenate(
        [one_hot((3 * t, n), 0, row_roles, row_at[s]) for s in range(2)], axis=1
    )
    for j in range(3):
        total = dot(spread, zbuf[j])
        g_own[j] = total[:t]
        g_on[j] = total[t : 2 * t].astype(BF16)
        g_off[j] = total[2 * t :].astype(BF16)

    def grad_copy(src, dst, i, device):
        return remote(src, dst, grad_send.at[i], grad_recv.at[i], device)

    on_copy = grad_copy(g_on, r_on_buf, 0, (r_on, c))
    on_copy.start()
    off_x = grad_copy(g_off.at[1], r_buf.at[0], 1, (r_off, c_x))
    off_far = grad_copy(g_off.at[2], r_buf.at[1], 2, (r_off, c_take))
    off_own = grad_copy(g_off.at[0], r_buf.at[2], 3, (r_off, c))
    for copy in (off_x, off_far, off_own):
        copy.start()
    on_copy.wait_recv()
    for j in (1, 2):
        g_sum[j - 1] = (g_own[j] + r_on_buf[j].astype(F32)).astype(BF16)
    sum_x = grad_copy(g_sum.at[0], r_buf.at[3], 4, (r, c_x))
    sum_far = grad_copy(g_sum.at[1], r_buf.at[4], 5, (r, c_take))
    sum_x.start()
    sum_far.start()
    mine = g_own[0] + r_on_buf[0].astype(F32)
    grads = (off_x, off_far, off_own, sum_x, sum_far)
    for copy in grads:
        copy.wait_recv()
    for i in range(5):
        mine = mine + r_buf[i].astype(F32)
    out[0] = mine[:, :t]
    out[1] = mine[:, t:]
    for copy in first + [meas_x, fwd_x, fwd_far, on_copy] + meas_own + meas_fwd + list(grads):
        copy.wait_send()


def per_device(n_r, n_c, tables, specimen, probe, measured, centers, counts, helpers):
    t = specimen.shape[1]
    modes, _, n, _ = probe.shape
    fwd, bwd = tables
    vmem = pl.BlockSpec(memory_space=pltpu.VMEM)
    smem = pl.BlockSpec(memory_space=pltpu.SMEM)
    hbm = pl.BlockSpec(memory_space=pl.ANY)
    dma = pltpu.SemaphoreType.DMA
    return pl.pallas_call(
        functools.partial(kernel, n_r, n_c),
        out_shape=jax.ShapeDtypeStruct(specimen.shape, F32),
        in_specs=[smem, smem, smem, vmem, vmem, hbm, hbm, hbm],
        out_specs=vmem,
        scratch_shapes=[
            pltpu.VMEM(probe.shape, F32),
            pltpu.VMEM((2 * n, 2 * n), BF16),
            pltpu.VMEM((2 * n, 2 * n), BF16),
            pltpu.VMEM((2, 8, 128), jnp.int32),
            pltpu.VMEM((9, t, 2 * t), BF16),
            pltpu.VMEM((n_c, n, n), BF16),
            pltpu.VMEM((modes * n, 2 * n), BF16),
            pltpu.VMEM((2 * n, modes * n), BF16),
            pltpu.VMEM((2, 2 * n, modes * n), F32),
            pltpu.VMEM((3, 2 * n, 2 * t), BF16),
            pltpu.VMEM((3, t, 2 * t), F32),
            pltpu.VMEM((3, t, 2 * t), BF16),
            pltpu.VMEM((3, t, 2 * t), BF16),
            pltpu.VMEM((2, t, 2 * t), BF16),
            pltpu.VMEM((3, t, 2 * t), BF16),
            pltpu.VMEM((5, t, 2 * t), BF16),
            dma((3,)),
            dma((2,)),
            dma((9,)),
            dma((9,)),
            dma((n_c,)),
            dma((n_c,)),
            dma((6,)),
            dma((6,)),
        ],
        compiler_params=pltpu.CompilerParams(
            collective_id=0, has_side_effects=True, vmem_limit_bytes=56 * 1024 * 1024
        ),
    )(
        centers.reshape(4),
        counts.reshape(1),
        helpers.reshape(2),
        specimen,
        measured.reshape(n, n),
        probe,
        fwd,
        bwd,
    )


def solution(mesh):
    n_r, n_c = mesh.shape["row"], mesh.shape["col"]

    def program(specimen, probe, measured, centers, counts, helpers):
        base = dft_blocks(probe.shape[-1])
        tables = (jnp.asarray(base, BF16), jnp.asarray(base.T, BF16))
        return jax.shard_map(
            functools.partial(per_device, n_r, n_c, tables),
            mesh=mesh,
            in_specs=(
                P(None, "row", "col"),
                P(),
                P("row", "col", None, None, None),
                P("row", "col", None, None),
                P("row", "col"),
                P("row", "col", None),
            ),
            out_specs=P(None, "row", "col"),
            check_vma=False,
        )(specimen, probe, measured, centers, counts, helpers)

    return program
```

time: 261 us -> 55.9 us (0.21)
  the two profiles are of different devices: /device:TPU:80 before, /device:TPU:2 now
where the time goes in v1:
time: 55.9 us; the launch traced here: 55.7 us
  Pallas kernels  52.2 us (93%)
  local copies, waits for them, and re-layouts  2.84 us (5%)
  between operations  0.66 us (1%)
    pallas_call x1, Pallas kernels, per_device(): pl.pallas_call(functools.partial(kernel, n_r, n_c), out_shape=jax.ShapeDt...  52.2 us
    unnamed x1, local copies, waits for them, and re-layouts  1.57 us
    reshape x1, local copies, waits for them, and re-layouts, per_device(): centers.reshape(4)  1.27 us

profile of v1, /device:TPU:2, one launch (start us, length us, event | category | flops | bytes accessed | tf_op | source)
XLA Modules:
  0.0 55.7 jit_solution(16438496119496936273)
XLA Ops:
  0.7 1.3 %reshape.12.centers = s32[4]{0:T(128)} reshape(s32[1,1,2,2]{3,2,1,0:T(2,128)} %param.11) | data formatting | bytes 32 | tf_op jit(solution)/shard_map/reshape | solution.py:327
  1.9 52.2 %shard_map.82 = f32[2,128,128]{2,1,0:T(8,128)} custom-call(s32[4]{0:T(128)} %reshape.12.centers, s32[1]{0:T(128)} %bitcast.3.counts, s32[2]{0:T(128)} %bitcast.5, f32[2,128,128]{2,1,0:T(8,128)} %spec.1, f32[256,256]{1,0:T(8,128)} %bitcast.4, f32[4,2,256,256]{3,2,1,0:T(8,128)} %probe_hbm.1, bf16[512,512]{1,0:T(8,128)(2,1)} %constant.4.clone.fwd_hbm, ...), custom_call_target="tpu_custom_call" | custom-call | tf_op jit(solution)/shard_map/pallas_call | solution.py:292
  54.1 1.6 %copy.11 = f32[2,128,128]{2,1,0:T(8,128)} copy(f32[2,128,128]{2,1,0:T(8,128)} %shard_map.82) | data formatting | bytes 262144

commit v2 on v1

--- a/solution.py
+++ b/solution.py
@@ -12,6 +12,7 @@
 MESH = pl.DeviceIdType.MESH
 F32 = jnp.float32
 BF16 = jnp.bfloat16
+CHUNKS = 4
 
 
 def dft_blocks(extent):
@@ -70,16 +71,22 @@
     odd_r, odd_c = lax.rem(r, 2), lax.rem(c, 2)
     r_on = r + 1 - 2 * odd_r
     r_off = lax.rem(r - 1 + 2 * odd_r + n_r, n_r)
+    inside = (r > 0) & (r < n_r - 1)
     c_x = c + 1 - 2 * odd_c
     c_give = lax.rem(c - 2 + 4 * odd_c + n_c, n_c)
     c_take = lax.rem(c + 2 - 4 * odd_c + n_c, n_c)
     peers = [lax.rem(c + 2 * k, n_c) for k in range(1, n_c // 2)]
 
     barrier = pltpu.get_barrier_semaphore()
-    partners = [(r_on, c), (r_off, c), (r, c_x), (r_off, c_x), (r_off, c_give), (r_off, c_take)]
-    partners += [(r, p) for p in peers]
-    for partner in partners:
-        pl.semaphore_signal(barrier, inc=1, device_id=partner, device_id_type=MESH)
+    near = [(r_on, c), (r, c_x)] + [(r, p) for p in peers]
+    across = [(r_off, c), (r_off, c_x), (r_off, c_give), (r_off, c_take)]
+
+    def greet(partners):
+        for partner in partners:
+            pl.semaphore_signal(barrier, inc=1, device_id=partner, device_id_type=MESH)
+
+    greet(near)
+    pl.when(inside)(lambda: greet(across))
 
     loads = [
         pltpu.make_async_copy(src, dst, local_sem.at[i])
@@ -89,15 +96,21 @@
         load.start()
 
     nb[0] = jnp.concatenate([spec[0], spec[1]], axis=1).astype(BF16)
-    values = [centers[0], centers[1], centers[2], centers[3], helpers[0], helpers[1], counts[0]]
+    values = [centers[0, 0, i, j] for i in range(2) for j in range(2)]
+    values += [helpers[0, 0, 0], helpers[0, 0, 1], counts[...]]
     which = lax.broadcasted_iota(jnp.int32, (8, 128), 0)
     block = jnp.zeros((8, 128), jnp.int32)
     for i, value in enumerate(values):
         block = jnp.where(which == i, value, block)
     meta[0] = block
-    meas[c] = measured[...].astype(BF16)
-
-    pl.semaphore_wait(barrier, len(partners))
+    meas[c] = measured[...].astype(BF16).reshape(meas.shape[1:])
+
+    @pl.when(jnp.logical_not(inside))
+    def _():
+        nb[6:9] = jnp.zeros((3, t, 2 * t), BF16)
+        r_buf[0:3] = jnp.zeros((3, t, 2 * t), BF16)
+
+    pl.semaphore_wait(barrier, len(near) + jnp.where(inside, len(across), 0))
 
     def remote(src, dst, send, recv, device):
         return pltpu.make_async_remote_copy(
@@ -119,17 +132,47 @@
     to_off = halo(0, 6, (r_off, c))
     to_on = halo(0, 3, (r_on, c))
     meta_copy = remote(meta.at[0], meta.at[1], meta_sem.at[0], meta_sem.at[1], (r, c_x))
-    first = [meta_copy, to_x, to_off_x, to_off_far, to_far, to_off, to_on]
-    for copy in first:
-        copy.start()
-    meas_x = remote(meas.at[c], meas.at[c], meas_send.at[0], meas_recv.at[0], (r, c_x))
-    meas_x.start()
-    meas_own = [
-        remote(meas.at[c], meas.at[c], meas_send.at[k + 1], meas_recv.at[k + 1], (r, p))
-        for k, p in enumerate(peers)
+    first = [meta_copy, to_x, to_far, to_on]
+    across_copies = [to_off_x, to_off_far, to_off]
+
+    def start(copies):
+        for copy in copies:
+            copy.start()
+
+    def wait_recv(copies):
+        for copy in copies:
+            copy.wait_recv()
+
+    def wait_send(copies):
+        for copy in copies:
+            copy.wait_send()
+
+    start(first[:2])
+    pl.when(inside)(lambda: start(across_copies))
+    start(first[2:])
+
+    chunks = meas.shape[1]
+    sides = n_c // 2 - 1
+
+    def meas_copy(src, sem, device):
+        return remote(src, src, meas_send.at[sem], meas_recv.at[sem], device)
+
+    meas_x = [meas_copy(meas.at[c, q], q, (r, c_x)) for q in range(chunks)]
+    meas_own = [meas_copy(meas.at[c], chunks + k, (r, p)) for k, p in enumerate(peers)]
+    meas_fwd = [
+        [
+            meas_copy(meas.at[c_x, q], chunks + sides * (q + 1) + k, (r, p))
+            for k, p in enumerate(peers)
+        ]
+        for q in range(chunks)
     ]
-    for copy in meas_own:
-        copy.start()
+    start(meas_x)
+    start(meas_own)
+
+    def pass_on(some):
+        for q in some:
+            meas_x[q].wait_recv()
+            start(meas_fwd[q])
 
     to_x.wait_recv()
     fwd_x = halo(1, 4, (r_on, c))
@@ -165,8 +208,8 @@
     col_roles = (col_own, t, col_far)
     row_at = [jnp.where(live[s], cr[s], 8 * n) for s in range(2)]
 
-    for copy in (to_off, to_off_x, to_off_far, to_on, fwd_x, fwd_far):
-        copy.wait_recv()
+    pl.when(inside)(lambda: wait_recv(across_copies))
+    wait_recv([to_on, fwd_x, fwd_far])
     for load in loads:
         load.wait()
 
@@ -193,22 +236,9 @@
             cols_buf[:n, k * n : (k + 1) * n] = half[:, :n]
             cols_buf[n:, k * n : (k + 1) * n] = half[:, n:]
         far[s] = dot(bwd[...], cols_buf[...])
-
-    meas_x.wait_recv()
-    meas_fwd = [
-        remote(
-            meas.at[c_x],
-            meas.at[c_x],
-            meas_send.at[n_c // 2 + k],
-            meas_recv.at[n_c // 2 + k],
-            (r, p),
-        )
-        for k, p in enumerate(peers)
-    ]
-    for copy in meas_fwd:
-        copy.start()
-    for copy in meas_own + meas_fwd:
-        copy.wait_recv()
+        pass_on(range(s * chunks // 2, (s + 1) * chunks // 2))
+
+    wait_recv(meas_own + sum(meas_fwd, []))
 
     for s in range(2):
         intensity = jnp.zeros((n, n), F32)
@@ -218,7 +248,7 @@
             intensity = intensity + (f_re * f_re + f_im * f_im)
         amp = jnp.zeros((n, n), F32)
         for h in range(n_c):
-            amp = amp + jnp.where(hc[s] == h, meas[h].astype(F32), 0.0)
+            amp = amp + jnp.where(hc[s] == h, meas[h].reshape(n, n).astype(F32), 0.0)
         factor = 1.0 - amp * lax.rsqrt(jnp.maximum(intensity, 0.25))
         for k in range(modes):
             for part in range(2):
@@ -260,8 +290,8 @@
     off_x = grad_copy(g_off.at[1], r_buf.at[0], 1, (r_off, c_x))
     off_far = grad_copy(g_off.at[2], r_buf.at[1], 2, (r_off, c_take))
     off_own = grad_copy(g_off.at[0], r_buf.at[2], 3, (r_off, c))
-    for copy in (off_x, off_far, off_own):
-        copy.start()
+    across_grads = [off_x, off_far, off_own]
+    pl.when(inside)(lambda: start(across_grads))
     on_copy.wait_recv()
     for j in (1, 2):
         g_sum[j - 1] = (g_own[j] + r_on_buf[j].astype(F32)).astype(BF16)
@@ -270,15 +300,15 @@
     sum_x.start()
     sum_far.start()
     mine = g_own[0] + r_on_buf[0].astype(F32)
-    grads = (off_x, off_far, off_own, sum_x, sum_far)
-    for copy in grads:
-        copy.wait_recv()
+    pl.when(inside)(lambda: wait_recv(across_grads))
+    wait_recv([sum_x, sum_far])
     for i in range(5):
         mine = mine + r_buf[i].astype(F32)
     out[0] = mine[:, :t]
     out[1] = mine[:, t:]
-    for copy in first + [meas_x, fwd_x, fwd_far, on_copy] + meas_own + meas_fwd + list(grads):
-        copy.wait_send()
+    wait_send(first + meas_x + [fwd_x, fwd_far, on_copy, sum_x, sum_far])
+    wait_send(meas_own + sum(meas_fwd, []))
+    pl.when(inside)(lambda: wait_send(across_copies + across_grads))
 
 
 def per_device(n_r, n_c, tables, specimen, probe, measured, centers, counts, helpers):
@@ -292,7 +322,7 @@
     return pl.pallas_call(
         functools.partial(kernel, n_r, n_c),
         out_shape=jax.ShapeDtypeStruct(specimen.shape, F32),
-        in_specs=[smem, smem, smem, vmem, vmem, hbm, hbm, hbm],
+        in_specs=[smem, vmem, smem, vmem, vmem, hbm, hbm, hbm],
         out_specs=vmem,
         scratch_shapes=[
             pltpu.VMEM(probe.shape, F32),
@@ -300,7 +330,7 @@
             pltpu.VMEM((2 * n, 2 * n), BF16),
             pltpu.VMEM((2, 8, 128), jnp.int32),
             pltpu.VMEM((9, t, 2 * t), BF16),
-            pltpu.VMEM((n_c, n, n), BF16),
+            pltpu.VMEM((n_c, CHUNKS, n // CHUNKS, n), BF16),
             pltpu.VMEM((modes * n, 2 * n), BF16),
             pltpu.VMEM((2 * n, modes * n), BF16),
             pltpu.VMEM((2, 2 * n, modes * n), F32),
@@ -315,8 +345,8 @@
             dma((2,)),
             dma((9,)),
             dma((9,)),
-            dma((n_c,)),
-            dma((n_c,)),
+            dma((CHUNKS + (CHUNKS + 1) * (n_c // 2 - 1),)),
+            dma((CHUNKS + (CHUNKS + 1) * (n_c // 2 - 1),)),
             dma((6,)),
             dma((6,)),
         ],
@@ -324,9 +354,9 @@
             collective_id=0, has_side_effects=True, vmem_limit_bytes=56 * 1024 * 1024
         ),
     )(
-        centers.reshape(4),
-        counts.reshape(1),
-        helpers.reshape(2),
+        centers,
+        counts,
+        helpers,
         specimen,
         measured.reshape(n, n),
         probe,

time: 55.9 us -> 49.6 us (0.89)
  the two profiles are of different devices: /device:TPU:2 before, /device:TPU:1 now
where the time goes in v2:
time: 49.6 us; the launch traced here: 49.4 us
  Pallas kernels  47.2 us (95%)
  local copies, waits for them, and re-layouts  1.57 us (3%)
  between operations  0.66 us (1%)
    pallas_call x1, Pallas kernels, per_device(): pl.pallas_call(functools.partial(kernel, n_r, n_c), out_shape=jax.ShapeDt...  47.2 us
    unnamed x1, local copies, waits for them, and re-layouts  1.57 us

profile of v2, /device:TPU:1, one launch (start us, length us, event | category | flops | bytes accessed | tf_op | source)
XLA Modules:
  0.0 49.4 jit_solution(6788880777069200242)
XLA Ops:
  0.7 47.2 %shard_map.82 = f32[2,128,128]{2,1,0:T(8,128)} custom-call(s32[1,1,2,2]{3,2,1,0:T(2,128)} %centers.1, s32[1,1]{1,0:T(1,128)S(6)} %copy.10.counts, s32[1,1,2]{2,1,0:T(1,128)} %helpers.1, f32[2,128,128]{2,1,0:T(8,128)} %spec.1, f32[256,256]{1,0:T(8,128)} %bitcast.1, f32[4,2,256,256]{3,2,1,0:T(8,128)} %probe_hbm.1, bf16[512,512]{1,0:T(8,128)(2,1)} %constant.4.clone.fwd_hbm, ...), custom_call_target="tpu_custom_call" | custom-call | tf_op jit(solution)/shard_map/pallas_call | solution.py:322
  47.8 1.6 %copy.11 = f32[2,128,128]{2,1,0:T(8,128)} copy(f32[2,128,128]{2,1,0:T(8,128)} %shard_map.82) | data formatting | bytes 262144

commit v3 on v2

--- a/solution.py
+++ b/solution.py
@@ -33,12 +33,14 @@
     centers,
     counts,
     helpers,
-    spec,
-    measured,
+    spec_hbm,
+    measured_hbm,
     probe_hbm,
     fwd_hbm,
     bwd_hbm,
     out,
+    spec,
+    measured,
     probe,
     fwd,
     bwd,
@@ -90,11 +92,20 @@
 
     loads = [
         pltpu.make_async_copy(src, dst, local_sem.at[i])
-        for i, (src, dst) in enumerate([(probe_hbm, probe), (fwd_hbm, fwd), (bwd_hbm, bwd)])
+        for i, (src, dst) in enumerate(
+            [
+                (spec_hbm, spec),
+                (measured_hbm, measured),
+                (probe_hbm, probe),
+                (fwd_hbm, fwd),
+                (bwd_hbm, bwd),
+            ]
+        )
     ]
     for load in loads:
         load.start()
 
+    loads[0].wait()
     nb[0] = jnp.concatenate([spec[0], spec[1]], axis=1).astype(BF16)
     values = [centers[0, 0, i, j] for i in range(2) for j in range(2)]
     values += [helpers[0, 0, 0], helpers[0, 0, 1], counts[...]]
@@ -103,6 +114,7 @@
     for i, value in enumerate(values):
         block = jnp.where(which == i, value, block)
     meta[0] = block
+    loads[1].wait()
     meas[c] = measured[...].astype(BF16).reshape(meas.shape[1:])
 
     @pl.when(jnp.logical_not(inside))
@@ -210,7 +222,7 @@
 
     pl.when(inside)(lambda: wait_recv(across_copies))
     wait_recv([to_on, fwd_x, fwd_far])
-    for load in loads:
+    for load in loads[2:]:
         load.wait()
 
     tiles = [jnp.concatenate([nb[j], nb[3 + j], nb[6 + j]], axis=0) for j in range(3)]
@@ -229,36 +241,46 @@
         re, im = patch[:n], patch[n:]
         for k in range(modes):
             p_re, p_im = probe[k, 0], probe[k, 1]
-            rows_buf[k * n : (k + 1) * n, :n] = (p_re * re - p_im * im).astype(BF16)
-            rows_buf[k * n : (k + 1) * n, n:] = (p_re * im + p_im * re).astype(BF16)
+            rows_buf[s, k * n : (k + 1) * n, :n] = (p_re * re - p_im * im).astype(BF16)
+            rows_buf[s, k * n : (k + 1) * n, n:] = (p_re * im + p_im * re).astype(BF16)
         for k in range(modes):
-            half = dot(rows_buf[k * n : (k + 1) * n], fwd[...]).astype(BF16)
-            cols_buf[:n, k * n : (k + 1) * n] = half[:, :n]
-            cols_buf[n:, k * n : (k + 1) * n] = half[:, n:]
-        far[s] = dot(bwd[...], cols_buf[...])
+            half = dot(rows_buf[s, k * n : (k + 1) * n], fwd[...]).astype(BF16)
+            cols_buf[s, :n, k * n : (k + 1) * n] = half[:, :n]
+            cols_buf[s, n:, k * n : (k + 1) * n] = half[:, n:]
+        far[s] = dot(bwd[...], cols_buf[s])
         pass_on(range(s * chunks // 2, (s + 1) * chunks // 2))
 
-    wait_recv(meas_own + sum(meas_fwd, []))
+    w = n // chunks
+    wait_recv(meas_own)
+    for q in range(chunks):
+        wait_recv(meas_fwd[q])
+        lo, block = q * w, modes * w
+        for s in range(2):
+            intensity = jnp.zeros((w, n), F32)
+            for k in range(modes):
+                f_re = far[s, lo : lo + w, k * n : (k + 1) * n]
+                f_im = far[s, n + lo : n + lo + w, k * n : (k + 1) * n]
+                intensity = intensity + (f_re * f_re + f_im * f_im)
+            amp = jnp.zeros((w, n), F32)
+            for h in range(n_c):
+                amp = amp + jnp.where(hc[s] == h, meas[h, q].astype(F32), 0.0)
+            factor = 1.0 - amp * lax.rsqrt(jnp.maximum(intensity, 0.25))
+            for k in range(modes):
+                at = q * block + k * w
+                for part in range(2):
+                    row = part * n + lo
+                    f = far[s, row : row + w, k * n : (k + 1) * n]
+                    rows_buf[s, at : at + w, part * n : (part + 1) * n] = (f * factor).astype(BF16)
+            back = dot(rows_buf[s, q * block : (q + 1) * block], bwd[...]).astype(BF16)
+            for k in range(modes):
+                for part in range(2):
+                    row = part * n + lo
+                    cols_buf[s, row : row + w, k * n : (k + 1) * n] = back[
+                        k * w : (k + 1) * w, part * n : (part + 1) * n
+                    ]
 
     for s in range(2):
-        intensity = jnp.zeros((n, n), F32)
-        for k in range(modes):
-            f_re = far[s, :n, k * n : (k + 1) * n]
-            f_im = far[s, n:, k * n : (k + 1) * n]
-            intensity = intensity + (f_re * f_re + f_im * f_im)
-        amp = jnp.zeros((n, n), F32)
-        for h in range(n_c):
-            amp = amp + jnp.where(hc[s] == h, meas[h].reshape(n, n).astype(F32), 0.0)
-        factor = 1.0 - amp * lax.rsqrt(jnp.maximum(intensity, 0.25))
-        for k in range(modes):
-            for part in range(2):
-                f = far[s, part * n : (part + 1) * n, k * n : (k + 1) * n]
-                rows_buf[k * n : (k + 1) * n, part * n : (part + 1) * n] = (f * factor).astype(BF16)
-        for k in range(modes):
-            back = dot(rows_buf[k * n : (k + 1) * n], bwd[...]).astype(BF16)
-            cols_buf[:n, k * n : (k + 1) * n] = back[:, :n]
-            cols_buf[n:, k * n : (k + 1) * n] = back[:, n:]
-        far[s] = dot(fwd[...], cols_buf[...])
+        far[s] = dot(fwd[...], cols_buf[s])
         g_re = jnp.zeros((n, n), F32)
         g_im = jnp.zeros((n, n), F32)
         for k in range(modes):
@@ -276,29 +298,31 @@
     spread = jnp.concatenate(
         [one_hot((3 * t, n), 0, row_roles, row_at[s]) for s in range(2)], axis=1
     )
-    for j in range(3):
-        total = dot(spread, zbuf[j])
-        g_own[j] = total[:t]
-        g_on[j] = total[t : 2 * t].astype(BF16)
-        g_off[j] = total[2 * t :].astype(BF16)
 
     def grad_copy(src, dst, i, device):
         return remote(src, dst, grad_send.at[i], grad_recv.at[i], device)
 
-    on_copy = grad_copy(g_on, r_on_buf, 0, (r_on, c))
-    on_copy.start()
-    off_x = grad_copy(g_off.at[1], r_buf.at[0], 1, (r_off, c_x))
-    off_far = grad_copy(g_off.at[2], r_buf.at[1], 2, (r_off, c_take))
-    off_own = grad_copy(g_off.at[0], r_buf.at[2], 3, (r_off, c))
+    order = (1, 2, 0)
+    on_copies = [grad_copy(g_on.at[j], r_on_buf.at[j], 5 + j, (r_on, c)) for j in range(3)]
+    for j in order:
+        g_on[j] = dot(spread[t : 2 * t], zbuf[j]).astype(BF16)
+        on_copies[j].start()
+    for j in order:
+        g_off[j] = dot(spread[2 * t :], zbuf[j]).astype(BF16)
+    off_x = grad_copy(g_off.at[1], r_buf.at[0], 0, (r_off, c_x))
+    off_far = grad_copy(g_off.at[2], r_buf.at[1], 1, (r_off, c_take))
+    off_own = grad_copy(g_off.at[0], r_buf.at[2], 2, (r_off, c))
     across_grads = [off_x, off_far, off_own]
     pl.when(inside)(lambda: start(across_grads))
-    on_copy.wait_recv()
-    for j in (1, 2):
+    for j in order:
+        g_own[j] = dot(spread[:t], zbuf[j])
+    sum_x = grad_copy(g_sum.at[0], r_buf.at[3], 3, (r, c_x))
+    sum_far = grad_copy(g_sum.at[1], r_buf.at[4], 4, (r, c_take))
+    for j, copy in ((1, sum_x), (2, sum_far)):
+        on_copies[j].wait_recv()
         g_sum[j - 1] = (g_own[j] + r_on_buf[j].astype(F32)).astype(BF16)
-    sum_x = grad_copy(g_sum.at[0], r_buf.at[3], 4, (r, c_x))
-    sum_far = grad_copy(g_sum.at[1], r_buf.at[4], 5, (r, c_take))
-    sum_x.start()
-    sum_far.start()
+        copy.start()
+    on_copies[0].wait_recv()
     mine = g_own[0] + r_on_buf[0].astype(F32)
     pl.when(inside)(lambda: wait_recv(across_grads))
     wait_recv([sum_x, sum_far])
@@ -306,7 +330,7 @@
         mine = mine + r_buf[i].astype(F32)
     out[0] = mine[:, :t]
     out[1] = mine[:, t:]
-    wait_send(first + meas_x + [fwd_x, fwd_far, on_copy, sum_x, sum_far])
+    wait_send(first + meas_x + [fwd_x, fwd_far, sum_x, sum_far] + on_copies)
     wait_send(meas_own + sum(meas_fwd, []))
     pl.when(inside)(lambda: wait_send(across_copies + across_grads))
 
@@ -322,17 +346,19 @@
     return pl.pallas_call(
         functools.partial(kernel, n_r, n_c),
         out_shape=jax.ShapeDtypeStruct(specimen.shape, F32),
-        in_specs=[smem, vmem, smem, vmem, vmem, hbm, hbm, hbm],
+        in_specs=[smem, vmem, smem, hbm, hbm, hbm, hbm, hbm],
         out_specs=vmem,
         scratch_shapes=[
+            pltpu.VMEM(specimen.shape, F32),
+            pltpu.VMEM((n, n), F32),
             pltpu.VMEM(probe.shape, F32),
             pltpu.VMEM((2 * n, 2 * n), BF16),
             pltpu.VMEM((2 * n, 2 * n), BF16),
             pltpu.VMEM((2, 8, 128), jnp.int32),
             pltpu.VMEM((9, t, 2 * t), BF16),
             pltpu.VMEM((n_c, CHUNKS, n // CHUNKS, n), BF16),
-            pltpu.VMEM((modes * n, 2 * n), BF16),
-            pltpu.VMEM((2 * n, modes * n), BF16),
+            pltpu.VMEM((2, modes * n, 2 * n), BF16),
+            pltpu.VMEM((2, 2 * n, modes * n), BF16),
             pltpu.VMEM((2, 2 * n, modes * n), F32),
             pltpu.VMEM((3, 2 * n, 2 * t), BF16),
             pltpu.VMEM((3, t, 2 * t), F32),
@@ -341,14 +367,14 @@
             pltpu.VMEM((2, t, 2 * t), BF16),
             pltpu.VMEM((3, t, 2 * t), BF16),
             pltpu.VMEM((5, t, 2 * t), BF16),
-            dma((3,)),
+            dma((5,)),
             dma((2,)),
             dma((9,)),
             dma((9,)),
             dma((CHUNKS + (CHUNKS + 1) * (n_c // 2 - 1),)),
             dma((CHUNKS + (CHUNKS + 1) * (n_c // 2 - 1),)),
-            dma((6,)),
-            dma((6,)),
+            dma((8,)),
+            dma((8,)),
         ],
         compiler_params=pltpu.CompilerParams(
             collective_id=0, has_side_effects=True, vmem_limit_bytes=56 * 1024 * 1024

time: 49.6 us -> 48.4 us (0.976)
  Pallas kernels: 47.2 us -> 46 us
    pallas_call x1, Pallas kernels: 47.2 us -> 46 us  [per_device(): pl.pallas_call(functools.partial(kernel, n_r, n_c), out_shape=jax.ShapeDt...]
where the time goes in v3:
time: 48.4 us; the launch traced here: 48.2 us
  Pallas kernels  46 us (95%)
  local copies, waits for them, and re-layouts  1.57 us (3%)
  between operations  0.66 us (1%)
    pallas_call x1, Pallas kernels, per_device(): pl.pallas_call(functools.partial(kernel, n_r, n_c), out_shape=jax.ShapeDt...  46 us
    unnamed x1, local copies, waits for them, and re-layouts  1.57 us

profile of v3, /device:TPU:1, one launch (start us, length us, event | category | flops | bytes accessed | tf_op | source)
XLA Modules:
  0.0 48.2 jit_solution(8231605148051332060)
XLA Ops:
  0.7 46.0 %shard_map.82 = f32[2,128,128]{2,1,0:T(8,128)} custom-call(s32[1,1,2,2]{3,2,1,0:T(2,128)} %centers.1, s32[1,1]{1,0:T(1,128)S(6)} %copy.10.counts, s32[1,1,2]{2,1,0:T(1,128)} %helpers.1, f32[2,128,128]{2,1,0:T(8,128)} %spec_hbm.1, f32[256,256]{1,0:T(8,128)} %bitcast.1, f32[4,2,256,256]{3,2,1,0:T(8,128)} %probe_hbm.1, bf16[512,512]{1,0:T(8,128)(2,1)} %constant.4.clone.fwd_hbm, ...), custom_call_target="tpu_custom_call" | custom-call | tf_op jit(solution)/shard_map/pallas_call | solution.py:346
  46.6 1.6 %copy.11 = f32[2,128,128]{2,1,0:T(8,128)} copy(f32[2,128,128]{2,1,0:T(8,128)} %shard_map.82) | data formatting | bytes 262144

commit v4 on v3

--- a/solution.py
+++ b/solution.py
@@ -345,7 +345,7 @@
     dma = pltpu.SemaphoreType.DMA
     return pl.pallas_call(
         functools.partial(kernel, n_r, n_c),
-        out_shape=jax.ShapeDtypeStruct(specimen.shape, F32),
+        out_shape=pltpu.VMEM(specimen.shape, F32),
         in_specs=[smem, vmem, smem, hbm, hbm, hbm, hbm, hbm],
         out_specs=vmem,
         scratch_shapes=[

time: 48.4 us -> 46.8 us (0.967)
  local copies, waits for them, and re-layouts: 1.57 us -> 0.66 us
  Pallas kernels: 46 us -> 45.3 us
    unnamed x1, local copies, waits for them, and re-layouts: 1.57 us -> 0.66 us
    pallas_call x1, Pallas kernels: 46 us -> 45.3 us  [per_device(): pl.pallas_call(functools.partial(kernel, n_r, n_c), out_shape=pltpu.VMEM(...]
where the time goes in v4:
time: 46.8 us; the launch traced here: 46.7 us
  Pallas kernels  45.3 us (97%)
  local copies, waits for them, and re-layouts  0.66 us (1%)
  between operations  0.66 us (1%)
    pallas_call x1, Pallas kernels, per_device(): pl.pallas_call(functools.partial(kernel, n_r, n_c), out_shape=pltpu.VMEM(...  45.3 us

profile of v4, /device:TPU:1, one launch (start us, length us, event | category | flops | bytes accessed | tf_op | source)
XLA Modules:
  0.0 46.7 jit_solution(2809500823437981422)
XLA Ops:
  0.7 45.3 %shard_map.82 = f32[2,128,128]{2,1,0:T(8,128)S(1)} custom-call(s32[1,1,2,2]{3,2,1,0:T(2,128)} %centers.1, s32[1,1]{1,0:T(1,128)S(6)} %copy.11.counts, s32[1,1,2]{2,1,0:T(1,128)} %helpers.1, f32[2,128,128]{2,1,0:T(8,128)} %spec_hbm.1, f32[256,256]{1,0:T(8,128)} %bitcast.1, f32[4,2,256,256]{3,2,1,0:T(8,128)} %probe_hbm.1, ...), custom_call_target="tpu_custom_call" | custom-call | tf_op jit(solution)/shard_map/pallas_call | solution.py:346
  46.0 0.7 %copy.10 = f32[2,128,128]{2,1,0:T(8,128)} copy(f32[2,128,128]{2,1,0:T(8,128)S(1)} %shard_map.82) | data formatting | bytes 262144

commit v5 on v4

--- a/solution.py
+++ b/solution.py
@@ -30,15 +30,18 @@
 def kernel(
     n_r,
     n_c,
-    centers,
-    counts,
-    helpers,
+    centers_hbm,
+    counts_hbm,
+    helpers_hbm,
     spec_hbm,
     measured_hbm,
     probe_hbm,
     fwd_hbm,
     bwd_hbm,
     out,
+    centers,
+    counts,
+    helpers,
     spec,
     measured,
     probe,
@@ -50,6 +53,7 @@
     rows_buf,
     cols_buf,
     far,
+    chi,
     zbuf,
     g_own,
     g_on,
@@ -95,6 +99,9 @@
         for i, (src, dst) in enumerate(
             [
                 (spec_hbm, spec),
+                (centers_hbm, centers),
+                (counts_hbm, counts),
+                (helpers_hbm, helpers),
                 (measured_hbm, measured),
                 (probe_hbm, probe),
                 (fwd_hbm, fwd),
@@ -107,14 +114,17 @@
 
     loads[0].wait()
     nb[0] = jnp.concatenate([spec[0], spec[1]], axis=1).astype(BF16)
-    values = [centers[0, 0, i, j] for i in range(2) for j in range(2)]
-    values += [helpers[0, 0, 0], helpers[0, 0, 1], counts[...]]
+    for load in loads[1:4]:
+        load.wait()
+    at, to = centers[0, 0], helpers[0]
+    values = [at[i : i + 1, j : j + 1] for i in range(2) for j in range(2)]
+    values += [to[:, 0:1], to[:, 1:2], counts[...]]
     which = lax.broadcasted_iota(jnp.int32, (8, 128), 0)
     block = jnp.zeros((8, 128), jnp.int32)
     for i, value in enumerate(values):
         block = jnp.where(which == i, value, block)
     meta[0] = block
-    loads[1].wait()
+    loads[4].wait()
     meas[c] = measured[...].astype(BF16).reshape(meas.shape[1:])
 
     @pl.when(jnp.logical_not(inside))
@@ -222,7 +232,7 @@
 
     pl.when(inside)(lambda: wait_recv(across_copies))
     wait_recv([to_on, fwd_x, fwd_far])
-    for load in loads[2:]:
+    for load in loads[5:]:
         load.wait()
 
     tiles = [jnp.concatenate([nb[j], nb[3 + j], nb[6 + j]], axis=0) for j in range(3)]
@@ -251,6 +261,10 @@
         pass_on(range(s * chunks // 2, (s + 1) * chunks // 2))
 
     w = n // chunks
+    halves = [
+        jnp.concatenate([fwd[:, i * t : (i + 1) * t], fwd[:, n + i * t : n + (i + 1) * t]], axis=1)
+        for i in range(2)
+    ]
     wait_recv(meas_own)
     for q in range(chunks):
         wait_recv(meas_fwd[q])
@@ -274,19 +288,23 @@
             back = dot(rows_buf[s, q * block : (q + 1) * block], bwd[...]).astype(BF16)
             for k in range(modes):
                 for part in range(2):
-                    row = part * n + lo
+                    row = lo // t * n + part * t + lo % t
                     cols_buf[s, row : row + w, k * n : (k + 1) * n] = back[
                         k * w : (k + 1) * w, part * n : (part + 1) * n
                     ]
 
+        if q == chunks // 2 - 1:
+            for s in range(2):
+                chi[s] = dot(halves[0], cols_buf[s, :n])
+
     for s in range(2):
-        far[s] = dot(fwd[...], cols_buf[s])
+        chi[s] = chi[s] + dot(halves[1], cols_buf[s, n:])
         g_re = jnp.zeros((n, n), F32)
         g_im = jnp.zeros((n, n), F32)
         for k in range(modes):
             p_re, p_im = probe[k, 0], probe[k, 1]
-            x_re = far[s, :n, k * n : (k + 1) * n]
-            x_im = far[s, n:, k * n : (k + 1) * n]
+            x_re = chi[s, :n, k * n : (k + 1) * n]
+            x_im = chi[s, n:, k * n : (k + 1) * n]
             g_re = g_re + (p_re * x_re + p_im * x_im)
             g_im = g_im + (p_re * x_im - p_im * x_re)
         grad = jnp.concatenate([g_re, g_im], axis=0).astype(BF16)
@@ -313,7 +331,7 @@
     off_far = grad_copy(g_off.at[2], r_buf.at[1], 1, (r_off, c_take))
     off_own = grad_copy(g_off.at[0], r_buf.at[2], 2, (r_off, c))
     across_grads = [off_x, off_far, off_own]
-    pl.when(inside)(lambda: start(across_grads))
+    pl.when(inside)(lambda: start(across_grads[:1]))
     for j in order:
         g_own[j] = dot(spread[:t], zbuf[j])
     sum_x = grad_copy(g_sum.at[0], r_buf.at[3], 3, (r, c_x))
@@ -322,6 +340,7 @@
         on_copies[j].wait_recv()
         g_sum[j - 1] = (g_own[j] + r_on_buf[j].astype(F32)).astype(BF16)
         copy.start()
+    pl.when(inside)(lambda: start(across_grads[1:]))
     on_copies[0].wait_recv()
     mine = g_own[0] + r_on_buf[0].astype(F32)
     pl.when(inside)(lambda: wait_recv(across_grads))
@@ -340,15 +359,17 @@
     modes, _, n, _ = probe.shape
     fwd, bwd = tables
     vmem = pl.BlockSpec(memory_space=pltpu.VMEM)
-    smem = pl.BlockSpec(memory_space=pltpu.SMEM)
     hbm = pl.BlockSpec(memory_space=pl.ANY)
     dma = pltpu.SemaphoreType.DMA
     return pl.pallas_call(
         functools.partial(kernel, n_r, n_c),
         out_shape=pltpu.VMEM(specimen.shape, F32),
-        in_specs=[smem, vmem, smem, hbm, hbm, hbm, hbm, hbm],
+        in_specs=[hbm] * 8,
         out_specs=vmem,
         scratch_shapes=[
+            pltpu.VMEM(centers.shape, jnp.int32),
+            pltpu.VMEM(counts.shape, jnp.int32),
+            pltpu.VMEM(helpers.shape, jnp.int32),
             pltpu.VMEM(specimen.shape, F32),
             pltpu.VMEM((n, n), F32),
             pltpu.VMEM(probe.shape, F32),
@@ -360,6 +381,7 @@
             pltpu.VMEM((2, modes * n, 2 * n), BF16),
             pltpu.VMEM((2, 2 * n, modes * n), BF16),
             pltpu.VMEM((2, 2 * n, modes * n), F32),
+            pltpu.VMEM((2, 2 * n, modes * n), F32),
             pltpu.VMEM((3, 2 * n, 2 * t), BF16),
             pltpu.VMEM((3, t, 2 * t), F32),
             pltpu.VMEM((3, t, 2 * t), BF16),
@@ -367,7 +389,7 @@
             pltpu.VMEM((2, t, 2 * t), BF16),
             pltpu.VMEM((3, t, 2 * t), BF16),
             pltpu.VMEM((5, t, 2 * t), BF16),
-            dma((5,)),
+            dma((8,)),
             dma((2,)),
             dma((9,)),
             dma((9,)),

time: 46.8 us -> 44.2 us (0.944)
  Pallas kernels: 45.3 us -> 42.8 us
    pallas_call x1, Pallas kernels: 45.3 us -> 42.8 us  [per_device(): pl.pallas_call(functools.partial(kernel, n_r, n_c), out_shape=pltpu.VMEM(...]
where the time goes in v5:
time: 44.2 us; the launch traced here: 44.1 us
  Pallas kernels  42.8 us (97%)
  local copies, waits for them, and re-layouts  0.66 us (1%)
  between operations  0.66 us (1%)
    pallas_call x1, Pallas kernels, per_device(): pl.pallas_call(functools.partial(kernel, n_r, n_c), out_shape=pltpu.VMEM(...  42.8 us

profile of v5, /device:TPU:1, one launch (start us, length us, event | category | flops | bytes accessed | tf_op | source)
XLA Modules:
  0.0 44.1 jit_solution(14211294584009135950)
XLA Ops:
  0.7 42.8 %shard_map.82 = f32[2,128,128]{2,1,0:T(8,128)S(1)} custom-call(s32[1,1,2,2]{3,2,1,0:T(2,128)} %centers_hbm.1, s32[1,1]{1,0:T(1,128)S(6)} %copy.11.counts_hbm, s32[1,1,2]{2,1,0:T(1,128)} %helpers_hbm.1, f32[2,128,128]{2,1,0:T(8,128)} %spec_hbm.1, f32[256,256]{1,0:T(8,128)} %bitcast.1, f32[4,2,256,256]{3,2,1,0:T(8,128)} %probe_hbm.1, ...), custom_call_target="tpu_custom_call" | custom-call | tf_op jit(solution)/shard_map/pallas_call | solution.py:364
  43.4 0.7 %copy.10 = f32[2,128,128]{2,1,0:T(8,128)} copy(f32[2,128,128]{2,1,0:T(8,128)S(1)} %shard_map.82) | data formatting | bytes 262144

commit v6 on v5

--- a/solution.py
+++ b/solution.py
@@ -78,6 +78,8 @@
     r_on = r + 1 - 2 * odd_r
     r_off = lax.rem(r - 1 + 2 * odd_r + n_r, n_r)
     inside = (r > 0) & (r < n_r - 1)
+    gives = (c > 0) & (c < n_c - 1)
+    takes = (c != 1) & (c != n_c - 2)
     c_x = c + 1 - 2 * odd_c
     c_give = lax.rem(c - 2 + 4 * odd_c + n_c, n_c)
     c_take = lax.rem(c + 2 - 4 * odd_c + n_c, n_c)
@@ -85,7 +87,7 @@
 
     barrier = pltpu.get_barrier_semaphore()
     near = [(r_on, c), (r, c_x)] + [(r, p) for p in peers]
-    across = [(r_off, c), (r_off, c_x), (r_off, c_give), (r_off, c_take)]
+    across = [(r_off, c), (r_off, c_x)]
 
     def greet(partners):
         for partner in partners:
@@ -93,6 +95,8 @@
 
     greet(near)
     pl.when(inside)(lambda: greet(across))
+    pl.when(inside & gives)(lambda: greet([(r_off, c_give)]))
+    pl.when(inside & takes)(lambda: greet([(r_off, c_take)]))
 
     loads = [
         pltpu.make_async_copy(src, dst, local_sem.at[i])
@@ -132,7 +136,18 @@
         nb[6:9] = jnp.zeros((3, t, 2 * t), BF16)
         r_buf[0:3] = jnp.zeros((3, t, 2 * t), BF16)
 
-    pl.semaphore_wait(barrier, len(near) + jnp.where(inside, len(across), 0))
+    @pl.when(jnp.logical_not(takes))
+    def _():
+        for i in (2, 5, 8):
+            nb[i] = jnp.zeros((t, 2 * t), BF16)
+
+    @pl.when(jnp.logical_not(gives))
+    def _():
+        for i in (1, 4):
+            r_buf[i] = jnp.zeros((t, 2 * t), BF16)
+
+    over = len(across) + jnp.where(gives, 1, 0) + jnp.where(takes, 1, 0)
+    pl.semaphore_wait(barrier, len(near) + jnp.where(inside, over, 0))
 
     def remote(src, dst, send, recv, device):
         return pltpu.make_async_remote_copy(
@@ -154,8 +169,8 @@
     to_off = halo(0, 6, (r_off, c))
     to_on = halo(0, 3, (r_on, c))
     meta_copy = remote(meta.at[0], meta.at[1], meta_sem.at[0], meta_sem.at[1], (r, c_x))
-    first = [meta_copy, to_x, to_far, to_on]
-    across_copies = [to_off_x, to_off_far, to_off]
+    first = [meta_copy, to_x, to_on]
+    across_copies = [to_off_x, to_off]
 
     def start(copies):
         for copy in copies:
@@ -171,6 +186,8 @@
 
     start(first[:2])
     pl.when(inside)(lambda: start(across_copies))
+    pl.when(inside & gives)(lambda: start([to_off_far]))
+    pl.when(gives)(lambda: start([to_far]))
     start(first[2:])
 
     chunks = meas.shape[1]
@@ -199,9 +216,13 @@
     to_x.wait_recv()
     fwd_x = halo(1, 4, (r_on, c))
     fwd_x.start()
-    to_far.wait_recv()
     fwd_far = halo(2, 5, (r_on, c))
-    fwd_far.start()
+
+    @pl.when(takes)
+    def _():
+        to_far.wait_recv()
+        fwd_far.start()
+
 
     meta_copy.wait_recv()
     info = meta[1]
@@ -231,7 +252,9 @@
     row_at = [jnp.where(live[s], cr[s], 8 * n) for s in range(2)]
 
     pl.when(inside)(lambda: wait_recv(across_copies))
-    wait_recv([to_on, fwd_x, fwd_far])
+    pl.when(inside & takes)(lambda: wait_recv([to_off_far]))
+    pl.when(takes)(lambda: wait_recv([fwd_far]))
+    wait_recv([to_on, fwd_x])
     for load in loads[5:]:
         load.wait()
 
@@ -330,26 +353,35 @@
     off_x = grad_copy(g_off.at[1], r_buf.at[0], 0, (r_off, c_x))
     off_far = grad_copy(g_off.at[2], r_buf.at[1], 1, (r_off, c_take))
     off_own = grad_copy(g_off.at[0], r_buf.at[2], 2, (r_off, c))
-    across_grads = [off_x, off_far, off_own]
-    pl.when(inside)(lambda: start(across_grads[:1]))
+    across_grads = [off_x, off_own]
+    pl.when(inside)(lambda: start([off_x]))
     for j in order:
         g_own[j] = dot(spread[:t], zbuf[j])
     sum_x = grad_copy(g_sum.at[0], r_buf.at[3], 3, (r, c_x))
     sum_far = grad_copy(g_sum.at[1], r_buf.at[4], 4, (r, c_take))
-    for j, copy in ((1, sum_x), (2, sum_far)):
+    for j in (1, 2):
         on_copies[j].wait_recv()
         g_sum[j - 1] = (g_own[j] + r_on_buf[j].astype(F32)).astype(BF16)
-        copy.start()
-    pl.when(inside)(lambda: start(across_grads[1:]))
+        if j == 1:
+            sum_x.start()
+    pl.when(takes)(lambda: start([sum_far]))
+    pl.when(inside & takes)(lambda: start([off_far]))
+    pl.when(inside)(lambda: start([off_own]))
     on_copies[0].wait_recv()
     mine = g_own[0] + r_on_buf[0].astype(F32)
     pl.when(inside)(lambda: wait_recv(across_grads))
-    wait_recv([sum_x, sum_far])
+    pl.when(inside & gives)(lambda: wait_recv([off_far]))
+    pl.when(gives)(lambda: wait_recv([sum_far]))
+    wait_recv([sum_x])
     for i in range(5):
         mine = mine + r_buf[i].astype(F32)
     out[0] = mine[:, :t]
     out[1] = mine[:, t:]
-    wait_send(first + meas_x + [fwd_x, fwd_far, sum_x, sum_far] + on_copies)
+    wait_send(first + meas_x + [fwd_x, sum_x] + on_copies)
+    pl.when(gives)(lambda: wait_send([to_far]))
+    pl.when(takes)(lambda: wait_send([fwd_far, sum_far]))
+    pl.when(inside & gives)(lambda: wait_send([to_off_far]))
+    pl.when(inside & takes)(lambda: wait_send([off_far]))
     wait_send(meas_own + sum(meas_fwd, []))
     pl.when(inside)(lambda: wait_send(across_copies + across_grads))
 

time: 44.2 us -> 43.7 us (0.989)
  Pallas kernels: 42.8 us -> 42.2 us
    pallas_call x1, Pallas kernels: 42.8 us -> 42.2 us  [per_device(): pl.pallas_call(functools.partial(kernel, n_r, n_c), out_shape=pltpu.VMEM(...]
where the time goes in v6:
time: 43.7 us; the launch traced here: 43.5 us
  Pallas kernels  42.2 us (97%)
  local copies, waits for them, and re-layouts  0.66 us (2%)
  between operations  0.66 us (2%)
    pallas_call x1, Pallas kernels, per_device(): pl.pallas_call(functools.partial(kernel, n_r, n_c), out_shape=pltpu.VMEM(...  42.2 us

profile of v6, /device:TPU:1, one launch (start us, length us, event | category | flops | bytes accessed | tf_op | source)
XLA Modules:
  0.0 43.5 jit_solution(8513277162847003636)
XLA Ops:
  0.7 42.2 %shard_map.82 = f32[2,128,128]{2,1,0:T(8,128)S(1)} custom-call(s32[1,1,2,2]{3,2,1,0:T(2,128)} %centers_hbm.1, s32[1,1]{1,0:T(1,128)S(6)} %copy.11.counts_hbm, s32[1,1,2]{2,1,0:T(1,128)} %helpers_hbm.1, f32[2,128,128]{2,1,0:T(8,128)} %spec_hbm.1, f32[256,256]{1,0:T(8,128)} %bitcast.1, f32[4,2,256,256]{3,2,1,0:T(8,128)} %probe_hbm.1, ...), custom_call_target="tpu_custom_call" | custom-call | tf_op jit(solution)/shard_map/pallas_call | solution.py:396
  42.9 0.7 %copy.10 = f32[2,128,128]{2,1,0:T(8,128)} copy(f32[2,128,128]{2,1,0:T(8,128)S(1)} %shard_map.82) | data formatting | bytes 262144

commit v7 on v6

--- a/solution.py
+++ b/solution.py
@@ -345,16 +345,17 @@
 
     order = (1, 2, 0)
     on_copies = [grad_copy(g_on.at[j], r_on_buf.at[j], 5 + j, (r_on, c)) for j in range(3)]
-    for j in order:
-        g_on[j] = dot(spread[t : 2 * t], zbuf[j]).astype(BF16)
-        on_copies[j].start()
-    for j in order:
-        g_off[j] = dot(spread[2 * t :], zbuf[j]).astype(BF16)
     off_x = grad_copy(g_off.at[1], r_buf.at[0], 0, (r_off, c_x))
     off_far = grad_copy(g_off.at[2], r_buf.at[1], 1, (r_off, c_take))
     off_own = grad_copy(g_off.at[0], r_buf.at[2], 2, (r_off, c))
     across_grads = [off_x, off_own]
+    g_on[1] = dot(spread[t : 2 * t], zbuf[1]).astype(BF16)
+    on_copies[1].start()
+    g_off[1] = dot(spread[2 * t :], zbuf[1]).astype(BF16)
     pl.when(inside)(lambda: start([off_x]))
+    for j in order[1:]:
+        g_on[j] = dot(spread[t : 2 * t], zbuf[j]).astype(BF16)
+        on_copies[j].start()
     for j in order:
         g_own[j] = dot(spread[:t], zbuf[j])
     sum_x = grad_copy(g_sum.at[0], r_buf.at[3], 3, (r, c_x))
@@ -364,6 +365,8 @@
         g_sum[j - 1] = (g_own[j] + r_on_buf[j].astype(F32)).astype(BF16)
         if j == 1:
             sum_x.start()
+            for i in order[1:]:
+                g_off[i] = dot(spread[2 * t :], zbuf[i]).astype(BF16)
     pl.when(takes)(lambda: start([sum_far]))
     pl.when(inside & takes)(lambda: start([off_far]))
     pl.when(inside)(lambda: start([off_own]))

time: 43.7 us -> 43.4 us (level)
  no operation moved by 1% of the time
where the time goes in v7:
time: 43.4 us; the launch traced here: 43.3 us
  Pallas kernels  41.9 us (97%)
  local copies, waits for them, and re-layouts  0.66 us (2%)
  between operations  0.66 us (2%)
    pallas_call x1, Pallas kernels, per_device(): pl.pallas_call(functools.partial(kernel, n_r, n_c), out_shape=pltpu.VMEM(...  41.9 us

profile of v7, /device:TPU:1, one launch (start us, length us, event | category | flops | bytes accessed | tf_op | source)
XLA Modules:
  0.0 43.3 jit_solution(9558292351723173023)
XLA Ops:
  0.7 41.9 %shard_map.82 = f32[2,128,128]{2,1,0:T(8,128)S(1)} custom-call(s32[1,1,2,2]{3,2,1,0:T(2,128)} %centers_hbm.1, s32[1,1]{1,0:T(1,128)S(6)} %copy.11.counts_hbm, s32[1,1,2]{2,1,0:T(1,128)} %helpers_hbm.1, f32[2,128,128]{2,1,0:T(8,128)} %spec_hbm.1, f32[256,256]{1,0:T(8,128)} %bitcast.1, f32[4,2,256,256]{3,2,1,0:T(8,128)} %probe_hbm.1, ...), custom_call_target="tpu_custom_call" | custom-call | tf_op jit(solution)/shard_map/pallas_call | solution.py:399
  42.6 0.7 %copy.10 = f32[2,128,128]{2,1,0:T(8,128)} copy(f32[2,128,128]{2,1,0:T(8,128)S(1)} %shard_map.82) | data formatting | bytes 262144
